TPU v7x, 512 devices: a whole 4x8x8 slice. The times are simulated.
512 devices in a mesh: band: 32 (over z_lo, y, core), dom: 16 (over z_hi, x).
Axes of the slice: x: 4, y: 8, z: 8 (z_hi: 4, z_lo: 2; z = z_hi * 2 + z_lo), core: 2. Of those that a mesh axis runs over, the one named last changes fastest.
Arguments:
- states: float32 [4096, 8, 128, 128], P('band', None, 'dom'), may hold values from -0.015625 to 0.015625
- window: float32 [128, 8, 128, 128], P('band', None, 'dom'), may hold values from -6 to 6
- potential: float32 [8, 128, 128], P(None, 'dom'), may hold values from -3 to 3
Outputs:
- intersection: float32 [4096, 128], P('band')
- hamiltonian: float32 [4096, 128], P('band')
All inputs are finite; a program needn't handle non-finite values.
Results may differ from a plain program's by a relative error of at most 0.00012.
Values sent between devices are 32-bit elements; how exact they have to be, the bound alone decides.
A program may use at most 64 MiB of HBM per device.

v0:
```python
import jax
import jax.numpy as jnp
from jax import lax
from jax.sharding import PartitionSpec as P

DEGREE = 4
coeffs = (
    -5369.0 / 1800.0,
    12.0 / 7.0,
    -15.0 / 56.0,
    10.0 / 189.0,
    -1.0 / 112.0,
    2.0 / 1925.0,
    -1.0 / 16632.0,
)
centre_value = 9.0
half_width = 7.0


def padded(block, sides, width):
    for axis, dim in sides:
        count = lax.axis_size(axis)
        forward = [(i, i + 1) for i in range(count - 1)]
        forward.append((count - 1, 0))
        backward = [(target, source) for source, target in forward]
        low = lax.ppermute(
            lax.slice_in_dim(block, block.shape[dim] - width, None, axis=dim), axis, forward
        )
        high = lax.ppermute(lax.slice_in_dim(block, 0, width, axis=dim), axis, backward)
        block = jnp.concatenate([low, block, high], axis=dim)
    return block


def stencil_sum(wave_in, padded_x, padded_y, potential):
    x_cells = wave_in.shape[2]
    y_cells = wave_in.shape[3]
    z_cells = wave_in.shape[1]
    along_z = jnp.pad(wave_in, ((0, 0), (6, 6), (0, 0), (0, 0)))
    laplace = 3.0 * coeffs[0] * wave_in
    for offset in range(1, 7):
        beside = (
            padded_x[:, :, 6 + offset : 6 + offset + x_cells]
            + padded_x[:, :, 6 - offset : 6 - offset + x_cells]
        )
        beside = (
            beside
            + padded_y[:, :, :, 6 + offset : 6 + offset + y_cells]
            + padded_y[:, :, :, 6 - offset : 6 - offset + y_cells]
        )
        beside = (
            beside
            + along_z[:, 6 + offset : 6 + offset + z_cells]
            + along_z[:, 6 - offset : 6 - offset + z_cells]
        )
        laplace = laplace + coeffs[offset] * beside
    return -0.5 * laplace + potential * wave_in


def apply_banded(wave_in, potential):
    padded_x = padded(wave_in, (("dom", 2),), 6)
    padded_y = jnp.concatenate((wave_in[:, :, :, -6:], wave_in, wave_in[:, :, :, :6]), axis=3)
    return stencil_sum(wave_in, padded_x, padded_y, potential)


def chebyshev(window, operate):
    previous = window
    current = (operate(window) - centre_value * window) / half_width
    for repeat_index in range(DEGREE - 1):
        following = 2.0 * (operate(current) - centre_value * current) / half_width - previous
        previous, current = (current, following)
    image = operate(current)
    return jnp.stack((current, image))


def per_device(states, window, potential):
    stacked = chebyshev(window, lambda wave: apply_banded(wave, potential))
    states_flat = states.reshape(states.shape[0], -1)
    whole_window = lax.all_gather(stacked, "band", axis=1, tiled=True)
    flat_piece = whole_window.reshape(-1, states_flat.shape[1])
    product = lax.dot_general(
        states_flat,
        flat_piece,
        (((1,), (1,)), ((), ())),
        precision=lax.Precision.HIGHEST,
        preferred_element_type=jnp.float32,
    )
    partial_value = product.reshape(states_flat.shape[0], 2, whole_window.shape[1])
    totals = lax.psum(partial_value, "dom")
    return (totals[:, 0, :], totals[:, 1, :])


def solution(mesh):
    in_specs = (P("band", None, "dom", None), P("band", None, "dom", None), P(None, "dom", None))
    out_specs = (P("band", None), P("band", None))
    return jax.shard_map(
        per_device, mesh=mesh, in_specs=in_specs, out_specs=out_specs, check_vma=False
    )
```

profile of v0, /device:TPU:8, one launch (start us, length us, event | category | flops | bytes accessed | tf_op | source)
XLA Modules:
  0.0 371.7 jit_solution(3588212571015930287)
XLA Ops:
  7.2 0.0 copy-start
  7.2 0.0 all-gather.2.cloned.1.call-start
  7.2 1.0 fusion.338
  8.2 13.1 %collective-permute-start = (f32[4,8,6,128]{3,2,1,0:T(8,128)S(1)}, f32[4,8,6,128]{3,2,1,0:T(8,128)S(1)}, u32[]{:S(2)}, u32[]{:S(2)}) collective-permute-start(f32[4,8,6,128]{3,2,1,0:T(8,128)S(1)} %get-tuple-element.22), channel_id=1, source_target_pairs={{1,0},{2,1},{3,2},{4,3},{5,4},{6,5},{7,6},{8,7},{9,8},{10,9},{11,1... | collective-permute-start | bytes 294920 | tf_op jit(solution)/shard_map/ppermute | solution.py:29
  21.4 1.9 collective-permute-start.1
  23.3 1.1 fusion.339
  24.4 0.8 broadcast_multiply_fusion.1
  25.1 0.9 constant_dynamic-update-slice_fusion.1
  26.1 0.8 collective-permute-done
  26.9 7.5 %collective-permute-done.1 = f32[4,8,6,128]{3,2,1,0:T(8,128)S(1)} collective-permute-done((f32[4,8,6,128]{3,2,1,0:T(8,128)S(1)}, f32[4,8,6,128]{3,2,1,0:T(8,128)S(1)}, u32[]{:S(2)}, u32[]{:S(2)}) %collective-permute-start.1) | collective-permute-done | bytes 98336 | tf_op jit(solution)/shard_map/ppermute | solution.py:26
  34.5 5.2 %broadcast_multiply_fusion = (f32[4,8,8,128]{3,2,1,0:T(8,128)S(1)}, f32[4,8,8,128]{3,2,1,0:T(8,128)S(1)}) fusion(f32[4,8,8,128]{3,2,1,0:T(8,128)} %param.4, f32[8,8,128]{2,1,0:T(8,128)} %param.5, f32[4,8,8,6]{3,2,1,0:T(8,128)S(1)} %get-tuple-element.25, f32[4,8,8,6]{3,2,1,0:T(8,128)S(1)} %get-tuple-element.24, ...), kind=kLoop, calls=%fused_computation.601 | loop fusion | flops 2195456 | bytes 1323008 | tf_op jit(solution)/shard_map/div | solution.py:67
  39.7 1.9 collective-permute-start.2
  41.6 3.9 %collective-permute-start.3 = (f32[4,8,6,128]{3,2,1,0:T(8,128)S(1)}, f32[4,8,6,128]{3,2,1,0:T(8,128)S(1)}, u32[]{:S(2)}, u32[]{:S(2)}) collective-permute-start(f32[4,8,6,128]{3,2,1,0:T(8,128)S(1)} %get-tuple-element.19), channel_id=1, source_target_pairs={{0,1},{1,2},{2,3},{3,4},{4,5},{5,6},{6,7},{7,8},{8,9},{9,10},{10,1... | collective-permute-start | bytes 294920 | tf_op jit(solution)/shard_map/ppermute | solution.py:26
  45.6 0.1 fusion.337
  45.7 1.8 collective-permute-done.2
  47.5 7.0 %collective-permute-done.3 = f32[4,8,6,128]{3,2,1,0:T(8,128)S(1)} collective-permute-done((f32[4,8,6,128]{3,2,1,0:T(8,128)S(1)}, f32[4,8,6,128]{3,2,1,0:T(8,128)S(1)}, u32[]{:S(2)}, u32[]{:S(2)}) %collective-permute-start.3) | collective-permute-done | bytes 98336 | tf_op jit(solution)/shard_map/ppermute | solution.py:26
  54.5 1.8 fusion.195
  56.2 1.9 collective-permute-start.4
  58.2 3.9 %collective-permute-start.5 = (f32[4,8,6,128]{3,2,1,0:T(8,128)S(1)}, f32[4,8,6,128]{3,2,1,0:T(8,128)S(1)}, u32[]{:S(2)}, u32[]{:S(2)}) collective-permute-start(f32[4,8,6,128]{3,2,1,0:T(8,128)S(1)} %get-tuple-element.15), channel_id=1, source_target_pairs={{0,1},{1,2},{2,3},{3,4},{4,5},{5,6},{6,7},{7,8},{8,9},{9,10},{10,1... | collective-permute-start | bytes 294920 | tf_op jit(solution)/shard_map/ppermute | solution.py:26
  62.1 0.1 fusion.335
  62.2 0.9 collective-permute-done.4
  63.1 6.2 %collective-permute-done.5 = f32[4,8,6,128]{3,2,1,0:T(8,128)S(1)} collective-permute-done((f32[4,8,6,128]{3,2,1,0:T(8,128)S(1)}, f32[4,8,6,128]{3,2,1,0:T(8,128)S(1)}, u32[]{:S(2)}, u32[]{:S(2)}) %collective-permute-start.5) | collective-permute-done | bytes 98336 | tf_op jit(solution)/shard_map/ppermute | solution.py:26
  69.3 1.6 fusion.134
  70.9 1.9 collective-permute-start.6
  72.9 3.9 %collective-permute-start.7 = (f32[4,8,6,128]{3,2,1,0:T(8,128)S(1)}, f32[4,8,6,128]{3,2,1,0:T(8,128)S(1)}, u32[]{:S(2)}, u32[]{:S(2)}) collective-permute-start(f32[4,8,6,128]{3,2,1,0:T(8,128)S(1)} %get-tuple-element.11), channel_id=1, source_target_pairs={{0,1},{1,2},{2,3},{3,4},{4,5},{5,6},{6,7},{7,8},{8,9},{9,10},{10,1... | collective-permute-start | bytes 294920 | tf_op jit(solution)/shard_map/ppermute | solution.py:26
  76.8 0.1 fusion.333
  76.9 0.9 collective-permute-done.6
  77.8 6.8 %collective-permute-done.7 = f32[4,8,6,128]{3,2,1,0:T(8,128)S(1)} collective-permute-done((f32[4,8,6,128]{3,2,1,0:T(8,128)S(1)}, f32[4,8,6,128]{3,2,1,0:T(8,128)S(1)}, u32[]{:S(2)}, u32[]{:S(2)}) %collective-permute-start.7) | collective-permute-done | bytes 98336 | tf_op jit(solution)/shard_map/ppermute | solution.py:26
  84.6 0.0 copy-done
  84.6 0.9 fusion.73
  85.5 1.9 collective-permute-start.8
  87.4 3.9 %collective-permute-start.9 = (f32[4,8,6,128]{3,2,1,0:T(8,128)S(1)}, f32[4,8,6,128]{3,2,1,0:T(8,128)S(1)}, u32[]{:S(2)}, u32[]{:S(2)}) collective-permute-start(f32[4,8,6,128]{3,2,1,0:T(8,128)S(1)} %get-tuple-element.7), channel_id=1, source_target_pairs={{0,1},{1,2},{2,3},{3,4},{4,5},{5,6},{6,7},{7,8},{8,9},{9,10},{10,1... | collective-permute-start | bytes 294920 | tf_op jit(solution)/shard_map/ppermute | solution.py:26
  91.3 0.1 fusion.331
  91.4 0.9 collective-permute-done.8
  92.3 6.1 %collective-permute-done.9 = f32[4,8,6,128]{3,2,1,0:T(8,128)S(1)} collective-permute-done((f32[4,8,6,128]{3,2,1,0:T(8,128)S(1)}, f32[4,8,6,128]{3,2,1,0:T(8,128)S(1)}, u32[]{:S(2)}, u32[]{:S(2)}) %collective-permute-start.9) | collective-permute-done | bytes 98336 | tf_op jit(solution)/shard_map/ppermute | solution.py:26
  98.5 0.9 fusion.12
  99.3 0.7 pad_maximum_fusion
  100.1 0.0 all-gather.2.cloned.1.call-update
  100.1 0.0 all-reduce.7.cloned.1.call-start
  100.1 69.7 %all-gather.2.cloned.1.call-done = f32[2,128,8,8,128]{4,3,2,1,0:T(8,128)} async-done(((f32[2,4,8,8,128]{4,3,2,1,0:T(8,128)}), f32[2,128,8,8,128]{4,3,2,1,0:T(8,128)}) %all-gather.2.cloned.1.call-update) | async-done | bytes 8388624 | tf_op jit(solution)/shard_map/all_gather | solution.py:78
  169.9 9.4 %reshape.14 = f32[256,8192]{1,0:T(8,128)} reshape(f32[2,128,8,8,128]{4,3,2,1,0:T(8,128)} %all-gather.2.cloned.1.call-done) | data formatting | bytes 16777216 | tf_op jit(solution)/shard_map/reshape | solution.py:79
  179.2 11.7 %fusion = f32[256,128]{1,0:T(8,128)S(1)} fusion(f32[256,8192]{1,0:T(8,128)} %reshape.14, f32[16,8,64,128]{3,2,1,0:T(8,128)} %bitcast.19), kind=kOutput, calls=%fused_computation | convolution fusion | flops 3221225472 | bytes 12713984 | tf_op jit(solution)/shard_map/dot_general | solution.py:80
  191.0 0.7 copy.5
  191.7 0.0 all-reduce.7.cloned.1.call-update
  191.7 171.6 %all-reduce.7.cloned.1.call-done = f32[128,2,128]{2,0,1:T(8,128)} async-done(((f32[128,2,128]{2,0,1:T(8,128)}), f32[128,2,128]{2,0,1:T(8,128)}) %all-reduce.7.cloned.1.call-update) | async-done | bytes 131088 | tf_op jit(solution)/shard_map/psum | solution.py:88
  363.4 1.5 slice_bitcast_fusion
  (5 shorter events, 0.1 us)
Async XLA Ops:
  7.2 77.4 %copy-start = (f32[8,8,128]{2,1,0:T(8,128)S(1)}, f32[8,8,128]{2,1,0:T(8,128)}, u32[]{:S(2)}) copy-start(f32[8,8,128]{2,1,0:T(8,128)} %param.5) | copy-start | bytes 98308
  7.2 162.7 %all-gather.2.cloned.1.call-start = ((), (), s32[]{:S(2)}) async-start(), calls=%async_computation | async-start | bytes 8650752 | tf_op jit(solution)/shard_map/all_gather | solution.py:78
  8.2 18.7 %collective-permute-start = (f32[4,8,6,128]{3,2,1,0:T(8,128)S(1)}, f32[4,8,6,128]{3,2,1,0:T(8,128)S(1)}, u32[]{:S(2)}, u32[]{:S(2)}) collective-permute-start(f32[4,8,6,128]{3,2,1,0:T(8,128)S(1)} %get-tuple-element.22), channel_id=1, source_target_pairs={{1,0},{2,1},{3,2},{4,3},{5,4},{6,5},{7,6},{8,7},{9,8},{10,9},{11,1... | collective-permute-start | bytes 294920 | tf_op jit(solution)/shard_map/ppermute | solution.py:29
  21.4 13.1 %collective-permute-start.1 = (f32[4,8,6,128]{3,2,1,0:T(8,128)S(1)}, f32[4,8,6,128]{3,2,1,0:T(8,128)S(1)}, u32[]{:S(2)}, u32[]{:S(2)}) collective-permute-start(f32[4,8,6,128]{3,2,1,0:T(8,128)S(1)} %get-tuple-element.23), channel_id=1, source_target_pairs={{0,1},{1,2},{2,3},{3,4},{4,5},{5,6},{6,7},{7,8},{8,9},{9,10},{10,1... | collective-permute-start | bytes 294920 | tf_op jit(solution)/shard_map/ppermute | solution.py:26
  39.7 7.8 %collective-permute-start.2 = (f32[4,8,6,128]{3,2,1,0:T(8,128)S(1)}, f32[4,8,6,128]{3,2,1,0:T(8,128)S(1)}, u32[]{:S(2)}, u32[]{:S(2)}) collective-permute-start(f32[4,8,6,128]{3,2,1,0:T(8,128)S(1)} %get-tuple-element.18), channel_id=1, source_target_pairs={{1,0},{2,1},{3,2},{4,3},{5,4},{6,5},{7,6},{8,7},{9,8},{10,9},{11,1... | collective-permute-start | bytes 294920 | tf_op jit(solution)/shard_map/ppermute | solution.py:29
  41.6 12.8 %collective-permute-start.3 = (f32[4,8,6,128]{3,2,1,0:T(8,128)S(1)}, f32[4,8,6,128]{3,2,1,0:T(8,128)S(1)}, u32[]{:S(2)}, u32[]{:S(2)}) collective-permute-start(f32[4,8,6,128]{3,2,1,0:T(8,128)S(1)} %get-tuple-element.19), channel_id=1, source_target_pairs={{0,1},{1,2},{2,3},{3,4},{4,5},{5,6},{6,7},{7,8},{8,9},{9,10},{10,1... | collective-permute-start | bytes 294920 | tf_op jit(solution)/shard_map/ppermute | solution.py:26
  56.2 6.9 %collective-permute-start.4 = (f32[4,8,6,128]{3,2,1,0:T(8,128)S(1)}, f32[4,8,6,128]{3,2,1,0:T(8,128)S(1)}, u32[]{:S(2)}, u32[]{:S(2)}) collective-permute-start(f32[4,8,6,128]{3,2,1,0:T(8,128)S(1)} %get-tuple-element.14), channel_id=1, source_target_pairs={{1,0},{2,1},{3,2},{4,3},{5,4},{6,5},{7,6},{8,7},{9,8},{10,9},{11,1... | collective-permute-start | bytes 294920 | tf_op jit(solution)/shard_map/ppermute | solution.py:29
  58.2 11.1 %collective-permute-start.5 = (f32[4,8,6,128]{3,2,1,0:T(8,128)S(1)}, f32[4,8,6,128]{3,2,1,0:T(8,128)S(1)}, u32[]{:S(2)}, u32[]{:S(2)}) collective-permute-start(f32[4,8,6,128]{3,2,1,0:T(8,128)S(1)} %get-tuple-element.15), channel_id=1, source_target_pairs={{0,1},{1,2},{2,3},{3,4},{4,5},{5,6},{6,7},{7,8},{8,9},{9,10},{10,1... | collective-permute-start | bytes 294920 | tf_op jit(solution)/shard_map/ppermute | solution.py:26
  70.9 6.9 %collective-permute-start.6 = (f32[4,8,6,128]{3,2,1,0:T(8,128)S(1)}, f32[4,8,6,128]{3,2,1,0:T(8,128)S(1)}, u32[]{:S(2)}, u32[]{:S(2)}) collective-permute-start(f32[4,8,6,128]{3,2,1,0:T(8,128)S(1)} %get-tuple-element.10), channel_id=1, source_target_pairs={{1,0},{2,1},{3,2},{4,3},{5,4},{6,5},{7,6},{8,7},{9,8},{10,9},{11,1... | collective-permute-start | bytes 294920 | tf_op jit(solution)/shard_map/ppermute | solution.py:29
  72.9 11.7 %collective-permute-start.7 = (f32[4,8,6,128]{3,2,1,0:T(8,128)S(1)}, f32[4,8,6,128]{3,2,1,0:T(8,128)S(1)}, u32[]{:S(2)}, u32[]{:S(2)}) collective-permute-start(f32[4,8,6,128]{3,2,1,0:T(8,128)S(1)} %get-tuple-element.11), channel_id=1, source_target_pairs={{0,1},{1,2},{2,3},{3,4},{4,5},{5,6},{6,7},{7,8},{8,9},{9,10},{10,1... | collective-permute-start | bytes 294920 | tf_op jit(solution)/shard_map/ppermute | solution.py:26
  85.5 6.9 %collective-permute-start.8 = (f32[4,8,6,128]{3,2,1,0:T(8,128)S(1)}, f32[4,8,6,128]{3,2,1,0:T(8,128)S(1)}, u32[]{:S(2)}, u32[]{:S(2)}) collective-permute-start(f32[4,8,6,128]{3,2,1,0:T(8,128)S(1)} %get-tuple-element.6), channel_id=1, source_target_pairs={{1,0},{2,1},{3,2},{4,3},{5,4},{6,5},{7,6},{8,7},{9,8},{10,9},{11,1... | collective-permute-start | bytes 294920 | tf_op jit(solution)/shard_map/ppermute | solution.py:29
  87.4 11.1 %collective-permute-start.9 = (f32[4,8,6,128]{3,2,1,0:T(8,128)S(1)}, f32[4,8,6,128]{3,2,1,0:T(8,128)S(1)}, u32[]{:S(2)}, u32[]{:S(2)}) collective-permute-start(f32[4,8,6,128]{3,2,1,0:T(8,128)S(1)} %get-tuple-element.7), channel_id=1, source_target_pairs={{0,1},{1,2},{2,3},{3,4},{4,5},{5,6},{6,7},{7,8},{8,9},{9,10},{10,1... | collective-permute-start | bytes 294920 | tf_op jit(solution)/shard_map/ppermute | solution.py:26
  100.1 263.3 %all-reduce.7.cloned.1.call-start = ((), (), s32[]{:S(2)}) async-start(), calls=%async_computation.1 | async-start | bytes 262144 | tf_op jit(solution)/shard_map/psum | solution.py:88
Sparse Core Ops, SparseCore 0:
  100.2 69.6 all-gather.1
  191.9 171.4 all-reduce.6
where the time goes:
time: 373 us; the launch traced here: 372 us
  waiting for transfers between devices  280 us (75%)
  starting transfers between devices  38.5 us (10%)
  local copies, waits for them, and re-layouts  15.1 us (4%)
  between operations  14.2 us (4%)
  other arithmetic  11.8 us (3%)
  matrix products  11.7 us (3%)
    psum x1, waiting for transfers between devices, per_device(): totals = lax.psum(partial_value, 'dom')  172 us
    all_gather x1, waiting for transfers between devices, per_device(): whole_window = lax.all_gather(stacked, 'band', axis=1, tiled=True)  69.7 us
    ppermute x5, waiting for transfers between devices, padded(): lax.ppermute(lax.slice_in_dim(block, block.shape[dim] - width, None, axis...  33.6 us
    ppermute x5, starting transfers between devices, padded(): lax.ppermute(lax.slice_in_dim(block, 0, width, axis=dim), axis, backward)  20.8 us
    ppermute x5, starting transfers between devices, padded(): lax.ppermute(lax.slice_in_dim(block, block.shape[dim] - width, None, axis...  17.6 us
    dot_general x1, matrix products, per_device(): lax.dot_general(states_flat, flat_piece, (((1,), (1,)), ((), ())), precis...  11.7 us
    reshape x1, local copies, waits for them, and re-layouts, per_device(): flat_piece = whole_window.reshape(-1, states_flat.shape[1])  9.36 us
  transfers between devices with their start and end apart: 12, of which 12 were waited for; matrix products, arithmetic and copies ran while one was open for 1% of the time, Pallas kernels for 0%

commit v1 on v0

--- a/solution.py
+++ b/solution.py
@@ -85,7 +85,7 @@
         preferred_element_type=jnp.float32,
     )
     partial_value = product.reshape(states_flat.shape[0], 2, whole_window.shape[1])
-    totals = lax.psum(partial_value, "dom")
+    totals = jnp.sum(lax.all_gather(partial_value, "dom"), axis=0)
     return (totals[:, 0, :], totals[:, 1, :])
 
 

time: 373 us -> 265 us (0.71)
  waiting for transfers between devices: 280 us -> 174 us
    psum x1 -> x0, waiting for transfers between devices: 172 us -> none  [per_device(): totals = lax.psum(partial_value, 'dom')]
    all_gather x0 -> x1, waiting for transfers between devices: none -> 64.8 us  [per_device(): totals = jnp.sum(lax.all_gather(partial_value, 'dom'), axis=0)]
where the time goes in v1:
time: 265 us; the launch traced here: 264 us
  waiting for transfers between devices  174 us (66%)
  starting transfers between devices  38.5 us (15%)
  local copies, waits for them, and re-layouts  14.2 us (5%)
  between operations  14.2 us (5%)
  other arithmetic  11.8 us (4%)
  matrix products  11.7 us (4%)
    all_gather x1, waiting for transfers between devices, per_device(): whole_window = lax.all_gather(stacked, 'band', axis=1, tiled=True)  69.7 us
    all_gather x1, waiting for transfers between devices, per_device(): totals = jnp.sum(lax.all_gather(partial_value, 'dom'), axis=0)  64.8 us
    ppermute x5, waiting for transfers between devices, padded(): lax.ppermute(lax.slice_in_dim(block, block.shape[dim] - width, None, axis...  33.6 us
    ppermute x5, starting transfers between devices, padded(): lax.ppermute(lax.slice_in_dim(block, 0, width, axis=dim), axis, backward)  20.8 us
    ppermute x5, starting transfers between devices, padded(): lax.ppermute(lax.slice_in_dim(block, block.shape[dim] - width, None, axis...  17.6 us
    dot_general x1, matrix products, per_device(): lax.dot_general(states_flat, flat_piece, (((1,), (1,)), ((), ())), precis...  11.7 us
    reshape x1, local copies, waits for them, and re-layouts, per_device(): flat_piece = whole_window.reshape(-1, states_flat.shape[1])  9.37 us
    ppermute x5, waiting for transfers between devices, padded(): lax.ppermute(lax.slice_in_dim(block, 0, width, axis=dim), axis, backward)  5.42 us
  transfers between devices with their start and end apart: 12, of which 12 were waited for; matrix products, arithmetic and copies ran while one was open for 1% of the time, Pallas kernels for 0%

profile of v1, /device:TPU:8, one launch (start us, length us, event | category | flops | bytes accessed | tf_op | source)
XLA Modules:
  0.0 264.1 jit_solution(17716834653075428853)
XLA Ops:
  7.2 0.0 copy-start
  7.2 0.0 copy-start.1
  7.2 0.0 all-gather.3.cloned.1.call-start
  7.2 1.0 fusion.338
  8.2 13.1 %collective-permute-start = (f32[4,8,6,128]{3,2,1,0:T(8,128)S(1)}, f32[4,8,6,128]{3,2,1,0:T(8,128)S(1)}, u32[]{:S(2)}, u32[]{:S(2)}) collective-permute-start(f32[4,8,6,128]{3,2,1,0:T(8,128)S(1)} %get-tuple-element.24), channel_id=1, source_target_pairs={{1,0},{2,1},{3,2},{4,3},{5,4},{6,5},{7,6},{8,7},{9,8},{10,9},{11,1... | collective-permute-start | bytes 294920 | tf_op jit(solution)/shard_map/ppermute | solution.py:29
  21.4 1.9 collective-permute-start.1
  23.3 1.1 fusion.339
  24.4 0.8 broadcast_multiply_fusion.1
  25.2 0.9 constant_dynamic-update-slice_fusion.1
  26.1 0.8 collective-permute-done
  26.9 7.5 %collective-permute-done.1 = f32[4,8,6,128]{3,2,1,0:T(8,128)S(1)} collective-permute-done((f32[4,8,6,128]{3,2,1,0:T(8,128)S(1)}, f32[4,8,6,128]{3,2,1,0:T(8,128)S(1)}, u32[]{:S(2)}, u32[]{:S(2)}) %collective-permute-start.1) | collective-permute-done | bytes 98336 | tf_op jit(solution)/shard_map/ppermute | solution.py:26
  34.5 5.2 %broadcast_multiply_fusion = (f32[4,8,8,128]{3,2,1,0:T(8,128)S(1)}, f32[4,8,8,128]{3,2,1,0:T(8,128)S(1)}) fusion(f32[4,8,8,128]{3,2,1,0:T(8,128)} %param.4, f32[8,8,128]{2,1,0:T(8,128)} %param.5, f32[4,8,8,6]{3,2,1,0:T(8,128)S(1)} %get-tuple-element.27, f32[4,8,8,6]{3,2,1,0:T(8,128)S(1)} %get-tuple-element.26, ...), kind=kLoop, calls=%fused_computation.601 | loop fusion | flops 2195456 | bytes 1323008 | tf_op jit(solution)/shard_map/div | solution.py:67
  39.7 1.9 collective-permute-start.2
  41.7 3.9 %collective-permute-start.3 = (f32[4,8,6,128]{3,2,1,0:T(8,128)S(1)}, f32[4,8,6,128]{3,2,1,0:T(8,128)S(1)}, u32[]{:S(2)}, u32[]{:S(2)}) collective-permute-start(f32[4,8,6,128]{3,2,1,0:T(8,128)S(1)} %get-tuple-element.21), channel_id=1, source_target_pairs={{0,1},{1,2},{2,3},{3,4},{4,5},{5,6},{6,7},{7,8},{8,9},{9,10},{10,1... | collective-permute-start | bytes 294920 | tf_op jit(solution)/shard_map/ppermute | solution.py:26
  45.6 0.1 fusion.337
  45.7 1.8 collective-permute-done.2
  47.5 7.0 %collective-permute-done.3 = f32[4,8,6,128]{3,2,1,0:T(8,128)S(1)} collective-permute-done((f32[4,8,6,128]{3,2,1,0:T(8,128)S(1)}, f32[4,8,6,128]{3,2,1,0:T(8,128)S(1)}, u32[]{:S(2)}, u32[]{:S(2)}) %collective-permute-start.3) | collective-permute-done | bytes 98336 | tf_op jit(solution)/shard_map/ppermute | solution.py:26
  54.5 0.0 copy-done
  54.5 0.9 fusion.195
  55.4 1.9 collective-permute-start.4
  57.3 3.9 %collective-permute-start.5 = (f32[4,8,6,128]{3,2,1,0:T(8,128)S(1)}, f32[4,8,6,128]{3,2,1,0:T(8,128)S(1)}, u32[]{:S(2)}, u32[]{:S(2)}) collective-permute-start(f32[4,8,6,128]{3,2,1,0:T(8,128)S(1)} %get-tuple-element.17), channel_id=1, source_target_pairs={{0,1},{1,2},{2,3},{3,4},{4,5},{5,6},{6,7},{7,8},{8,9},{9,10},{10,1... | collective-permute-start | bytes 294920 | tf_op jit(solution)/shard_map/ppermute | solution.py:26
  61.2 0.1 fusion.335
  61.3 0.9 collective-permute-done.4
  62.3 6.2 %collective-permute-done.5 = f32[4,8,6,128]{3,2,1,0:T(8,128)S(1)} collective-permute-done((f32[4,8,6,128]{3,2,1,0:T(8,128)S(1)}, f32[4,8,6,128]{3,2,1,0:T(8,128)S(1)}, u32[]{:S(2)}, u32[]{:S(2)}) %collective-permute-start.5) | collective-permute-done | bytes 98336 | tf_op jit(solution)/shard_map/ppermute | solution.py:26
  68.4 0.0 copy-done.1
  68.4 0.9 fusion.134
  69.3 1.9 collective-permute-start.6
  71.2 3.9 %collective-permute-start.7 = (f32[4,8,6,128]{3,2,1,0:T(8,128)S(1)}, f32[4,8,6,128]{3,2,1,0:T(8,128)S(1)}, u32[]{:S(2)}, u32[]{:S(2)}) collective-permute-start(f32[4,8,6,128]{3,2,1,0:T(8,128)S(1)} %get-tuple-element.13), channel_id=1, source_target_pairs={{0,1},{1,2},{2,3},{3,4},{4,5},{5,6},{6,7},{7,8},{8,9},{9,10},{10,1... | collective-permute-start | bytes 294920 | tf_op jit(solution)/shard_map/ppermute | solution.py:26
  75.2 0.1 fusion.333
  75.3 0.9 collective-permute-done.6
  76.2 6.8 %collective-permute-done.7 = f32[4,8,6,128]{3,2,1,0:T(8,128)S(1)} collective-permute-done((f32[4,8,6,128]{3,2,1,0:T(8,128)S(1)}, f32[4,8,6,128]{3,2,1,0:T(8,128)S(1)}, u32[]{:S(2)}, u32[]{:S(2)}) %collective-permute-start.7) | collective-permute-done | bytes 98336 | tf_op jit(solution)/shard_map/ppermute | solution.py:26
  83.0 0.9 fusion.73
  83.8 1.9 collective-permute-start.8
  85.8 3.9 %collective-permute-start.9 = (f32[4,8,6,128]{3,2,1,0:T(8,128)S(1)}, f32[4,8,6,128]{3,2,1,0:T(8,128)S(1)}, u32[]{:S(2)}, u32[]{:S(2)}) collective-permute-start(f32[4,8,6,128]{3,2,1,0:T(8,128)S(1)} %get-tuple-element.9), channel_id=1, source_target_pairs={{0,1},{1,2},{2,3},{3,4},{4,5},{5,6},{6,7},{7,8},{8,9},{9,10},{10,1... | collective-permute-start | bytes 294920 | tf_op jit(solution)/shard_map/ppermute | solution.py:26
  89.7 0.1 fusion.331
  89.8 0.9 collective-permute-done.8
  90.7 6.1 %collective-permute-done.9 = f32[4,8,6,128]{3,2,1,0:T(8,128)S(1)} collective-permute-done((f32[4,8,6,128]{3,2,1,0:T(8,128)S(1)}, f32[4,8,6,128]{3,2,1,0:T(8,128)S(1)}, u32[]{:S(2)}, u32[]{:S(2)}) %collective-permute-start.9) | collective-permute-done | bytes 98336 | tf_op jit(solution)/shard_map/ppermute | solution.py:26
  96.8 0.9 fusion.12
  97.7 0.8 pad_maximum_fusion
  98.4 0.0 all-gather.3.cloned.1.call-update
  98.5 0.0 all-gather.5.cloned.1.call-start
  98.5 69.7 %all-gather.3.cloned.1.call-done = f32[2,128,8,8,128]{4,3,2,1,0:T(8,128)} async-done(((f32[2,4,8,8,128]{4,3,2,1,0:T(8,128)}), f32[2,128,8,8,128]{4,3,2,1,0:T(8,128)}) %all-gather.3.cloned.1.call-update) | async-done | bytes 8388624 | tf_op jit(solution)/shard_map/all_gather | solution.py:78
  168.2 9.4 %reshape.11 = f32[256,8192]{1,0:T(8,128)} reshape(f32[2,128,8,8,128]{4,3,2,1,0:T(8,128)} %all-gather.3.cloned.1.call-done) | data formatting | bytes 16777216 | tf_op jit(solution)/shard_map/reshape | solution.py:79
  177.6 11.7 %fusion = f32[256,128]{1,0:T(8,128)S(1)} fusion(f32[256,8192]{1,0:T(8,128)} %reshape.11, f32[16,8,64,128]{3,2,1,0:T(8,128)} %bitcast.21), kind=kOutput, calls=%fused_computation | convolution fusion | flops 3221225472 | bytes 12713984 | tf_op jit(solution)/shard_map/dot_general | solution.py:80
  189.3 0.7 copy.5
  190.1 0.0 all-gather.5.cloned.1.call-update
  190.1 64.8 %all-gather.5.cloned.1.call-done = f32[16,128,2,128]{3,1,2,0:T(8,128)} async-done(((f32[1,128,2,128]{3,1,2,0:T(8,128)}), f32[16,128,2,128]{3,1,2,0:T(8,128)}) %all-gather.5.cloned.1.call-update) | async-done | bytes 2097168 | tf_op jit(solution)/shard_map/all_gather | solution.py:88
  254.9 1.7 reduce_sum.9
  256.6 0.7 slice_bitcast_fusion
  (5 shorter events, 0.1 us)
Async XLA Ops:
  7.2 47.3 %copy-start = (f32[4,8,8,128]{3,2,1,0:T(8,128)S(1)}, f32[4,8,8,128]{3,2,1,0:T(8,128)}, u32[]{:S(2)}) copy-start(f32[4,8,8,128]{3,2,1,0:T(8,128)} %param.4) | copy-start | bytes 393220
  7.2 61.2 %copy-start.1 = (f32[8,8,128]{2,1,0:T(8,128)S(1)}, f32[8,8,128]{2,1,0:T(8,128)}, u32[]{:S(2)}) copy-start(f32[8,8,128]{2,1,0:T(8,128)} %param.5) | copy-start | bytes 98308
  7.2 161.1 %all-gather.3.cloned.1.call-start = ((), (), s32[]{:S(2)}) async-start(), calls=%async_computation | async-start | bytes 8650752 | tf_op jit(solution)/shard_map/all_gather | solution.py:78
  8.2 18.7 %collective-permute-start = (f32[4,8,6,128]{3,2,1,0:T(8,128)S(1)}, f32[4,8,6,128]{3,2,1,0:T(8,128)S(1)}, u32[]{:S(2)}, u32[]{:S(2)}) collective-permute-start(f32[4,8,6,128]{3,2,1,0:T(8,128)S(1)} %get-tuple-element.24), channel_id=1, source_target_pairs={{1,0},{2,1},{3,2},{4,3},{5,4},{6,5},{7,6},{8,7},{9,8},{10,9},{11,1... | collective-permute-start | bytes 294920 | tf_op jit(solution)/shard_map/ppermute | solution.py:29
  21.4 13.1 %collective-permute-start.1 = (f32[4,8,6,128]{3,2,1,0:T(8,128)S(1)}, f32[4,8,6,128]{3,2,1,0:T(8,128)S(1)}, u32[]{:S(2)}, u32[]{:S(2)}) collective-permute-start(f32[4,8,6,128]{3,2,1,0:T(8,128)S(1)} %get-tuple-element.25), channel_id=1, source_target_pairs={{0,1},{1,2},{2,3},{3,4},{4,5},{5,6},{6,7},{7,8},{8,9},{9,10},{10,1... | collective-permute-start | bytes 294920 | tf_op jit(solution)/shard_map/ppermute | solution.py:26
  39.7 7.8 %collective-permute-start.2 = (f32[4,8,6,128]{3,2,1,0:T(8,128)S(1)}, f32[4,8,6,128]{3,2,1,0:T(8,128)S(1)}, u32[]{:S(2)}, u32[]{:S(2)}) collective-permute-start(f32[4,8,6,128]{3,2,1,0:T(8,128)S(1)} %get-tuple-element.20), channel_id=1, source_target_pairs={{1,0},{2,1},{3,2},{4,3},{5,4},{6,5},{7,6},{8,7},{9,8},{10,9},{11,1... | collective-permute-start | bytes 294920 | tf_op jit(solution)/shard_map/ppermute | solution.py:29
  41.7 12.8 %collective-permute-start.3 = (f32[4,8,6,128]{3,2,1,0:T(8,128)S(1)}, f32[4,8,6,128]{3,2,1,0:T(8,128)S(1)}, u32[]{:S(2)}, u32[]{:S(2)}) collective-permute-start(f32[4,8,6,128]{3,2,1,0:T(8,128)S(1)} %get-tuple-element.21), channel_id=1, source_target_pairs={{0,1},{1,2},{2,3},{3,4},{4,5},{5,6},{6,7},{7,8},{8,9},{9,10},{10,1... | collective-permute-start | bytes 294920 | tf_op jit(solution)/shard_map/ppermute | solution.py:26
  55.4 6.9 %collective-permute-start.4 = (f32[4,8,6,128]{3,2,1,0:T(8,128)S(1)}, f32[4,8,6,128]{3,2,1,0:T(8,128)S(1)}, u32[]{:S(2)}, u32[]{:S(2)}) collective-permute-start(f32[4,8,6,128]{3,2,1,0:T(8,128)S(1)} %get-tuple-element.16), channel_id=1, source_target_pairs={{1,0},{2,1},{3,2},{4,3},{5,4},{6,5},{7,6},{8,7},{9,8},{10,9},{11,1... | collective-permute-start | bytes 294920 | tf_op jit(solution)/shard_map/ppermute | solution.py:29
  57.3 11.1 %collective-permute-start.5 = (f32[4,8,6,128]{3,2,1,0:T(8,128)S(1)}, f32[4,8,6,128]{3,2,1,0:T(8,128)S(1)}, u32[]{:S(2)}, u32[]{:S(2)}) collective-permute-start(f32[4,8,6,128]{3,2,1,0:T(8,128)S(1)} %get-tuple-element.17), channel_id=1, source_target_pairs={{0,1},{1,2},{2,3},{3,4},{4,5},{5,6},{6,7},{7,8},{8,9},{9,10},{10,1... | collective-permute-start | bytes 294920 | tf_op jit(solution)/shard_map/ppermute | solution.py:26
  69.3 6.9 %collective-permute-start.6 = (f32[4,8,6,128]{3,2,1,0:T(8,128)S(1)}, f32[4,8,6,128]{3,2,1,0:T(8,128)S(1)}, u32[]{:S(2)}, u32[]{:S(2)}) collective-permute-start(f32[4,8,6,128]{3,2,1,0:T(8,128)S(1)} %get-tuple-element.12), channel_id=1, source_target_pairs={{1,0},{2,1},{3,2},{4,3},{5,4},{6,5},{7,6},{8,7},{9,8},{10,9},{11,1... | collective-permute-start | bytes 294920 | tf_op jit(solution)/shard_map/ppermute | solution.py:29
  71.2 11.7 %collective-permute-start.7 = (f32[4,8,6,128]{3,2,1,0:T(8,128)S(1)}, f32[4,8,6,128]{3,2,1,0:T(8,128)S(1)}, u32[]{:S(2)}, u32[]{:S(2)}) collective-permute-start(f32[4,8,6,128]{3,2,1,0:T(8,128)S(1)} %get-tuple-element.13), channel_id=1, source_target_pairs={{0,1},{1,2},{2,3},{3,4},{4,5},{5,6},{6,7},{7,8},{8,9},{9,10},{10,1... | collective-permute-start | bytes 294920 | tf_op jit(solution)/shard_map/ppermute | solution.py:26
  83.8 6.9 %collective-permute-start.8 = (f32[4,8,6,128]{3,2,1,0:T(8,128)S(1)}, f32[4,8,6,128]{3,2,1,0:T(8,128)S(1)}, u32[]{:S(2)}, u32[]{:S(2)}) collective-permute-start(f32[4,8,6,128]{3,2,1,0:T(8,128)S(1)} %get-tuple-element.8), channel_id=1, source_target_pairs={{1,0},{2,1},{3,2},{4,3},{5,4},{6,5},{7,6},{8,7},{9,8},{10,9},{11,1... | collective-permute-start | bytes 294920 | tf_op jit(solution)/shard_map/ppermute | solution.py:29
  85.8 11.1 %collective-permute-start.9 = (f32[4,8,6,128]{3,2,1,0:T(8,128)S(1)}, f32[4,8,6,128]{3,2,1,0:T(8,128)S(1)}, u32[]{:S(2)}, u32[]{:S(2)}) collective-permute-start(f32[4,8,6,128]{3,2,1,0:T(8,128)S(1)} %get-tuple-element.9), channel_id=1, source_target_pairs={{0,1},{1,2},{2,3},{3,4},{4,5},{5,6},{6,7},{7,8},{8,9},{9,10},{10,1... | collective-permute-start | bytes 294920 | tf_op jit(solution)/shard_map/ppermute | solution.py:26
  98.5 156.4 %all-gather.5.cloned.1.call-start = ((), (), s32[]{:S(2)}) async-start(), calls=%async_computation.1 | async-start | bytes 2228224 | tf_op jit(solution)/shard_map/all_gather | solution.py:88
Sparse Core Ops, SparseCore 0:
  98.6 69.6 all-gather.2
  190.2 64.5 all-gather.4
